TPU v7x, 256 devices: a whole 4x4x8 slice. The times are simulated.
256 devices in a mesh: feat: 64 (over x, z, core), node: 4 (over y).
Axes of the slice: x: 4, y: 4, z: 8, core: 2. Of those that a mesh axis runs over, the one named last changes fastest.
Arguments:
- features: bfloat16 [32768, 1024], P(None, 'feat'), may hold values from -6 to 6
- w_self: bfloat16 [1024, 256], P('feat'), may hold values from -0.1875 to 0.1875
- w_neigh: bfloat16 [1024, 256], P('feat'), may hold values from -0.75 to 0.75
- bias: float32 [256], replicated, may hold values from -3 to 3
- d_out: bfloat16 [32768, 256], P(('node', 'feat')), may hold values from -6 to 6
- nbr_ids: int32 [256, 16], P('node'), may hold values from 0 to 255, as said below
- nbr_count: int32 [256], P('node'), may hold values from 1 to 16, as said below
- tiles: int32 [256, 16, 8, 128], P('node'), may hold values from 0 to 65535, as said below
Outputs:
- activated: bfloat16 [32768, 256], P(('node', 'feat'))
- grad_features: float32 [32768, 1024], P('node', 'feat')
- grad_self: float32 [1024, 256], P('feat')
- grad_neigh: float32 [1024, 256], P('feat')
Inputs may be any that keep to these rules, and one draw needn't show every extreme that they name: `nbr_ids`: the ids of one block row are distinct; only the first nbr_count slots of a row are live, the others hold ids and tiles that must be ignored. `nbr_count`: some block row of every draw has exactly 16 live slots. `tiles`: bits for destination rows 128 and above are zero; some destination nodes have no edges at all.
All inputs are finite; a program needn't handle non-finite values.
Results may differ from a plain program's by a relative error of at most 0.0075.
Values may be sent and summed in bfloat16 or wider, within the bound.
A program may use at most 64 MiB of HBM per device.

v0:
```python
import math
import jax
import jax.numpy as jnp
from jax import lax
from jax.sharding import PartitionSpec as P


def unpack(packed):
    shifts = jnp.arange(16, dtype=jnp.int32)
    bit_planes = jnp.bitwise_and(jnp.right_shift(packed[..., :, None, :], shifts[:, None]), 1)
    flat_shape = packed.shape[:-2] + (packed.shape[-2] * 16, packed.shape[-1])
    return bit_planes.reshape(flat_shape)


def shards(features, w_self, w_neigh, bias, d_out, nbr_ids, nbr_count, tiles):
    node_total = features.shape[0]
    feat_cols = features.shape[1]
    block_size = tiles.shape[3]
    blocks_here = nbr_ids.shape[0]
    group_rows = blocks_here * block_size
    all_blocks = node_total // block_size
    slot_total = nbr_ids.shape[1]
    node_group = lax.axis_index("node")
    blocked = features.reshape(all_blocks, block_size, feat_cols)

    def slot_tiles(slot_idx):
        packed = lax.dynamic_index_in_dim(tiles, slot_idx, 1, keepdims=False)
        block_ids = lax.dynamic_index_in_dim(nbr_ids, slot_idx, 1, keepdims=False)
        live_mask = (slot_idx < nbr_count).astype(jnp.float32)
        adjacency = unpack(packed).astype(jnp.bfloat16)
        return (adjacency, block_ids, live_mask)

    def forward_slot(slot_idx, state_pair):
        neigh_sum, degree = state_pair
        adjacency, block_ids, live_mask = slot_tiles(slot_idx)
        source = blocked[block_ids]
        product = jnp.einsum("bij,bjc->bic", adjacency, source, preferred_element_type=jnp.float32)
        neigh_sum = neigh_sum + product * live_mask[:, None, None]
        degree = degree + jnp.sum(adjacency, axis=2, dtype=jnp.float32) * live_mask[:, None]
        return (neigh_sum, degree)

    neigh_sum, degree = lax.fori_loop(
        0,
        slot_total,
        forward_slot,
        (
            jnp.zeros((blocks_here, block_size, feat_cols), jnp.float32),
            jnp.zeros((blocks_here, block_size), jnp.float32),
        ),
    )
    denom = jnp.maximum(degree, 1.0)
    neigh_mean = (neigh_sum / denom[..., None]).astype(jnp.bfloat16).reshape(group_rows, feat_cols)
    own_rows = lax.dynamic_slice_in_dim(features, node_group * group_rows, group_rows, 0)
    pre_act = (
        lax.psum_scatter(
            jnp.dot(own_rows, w_self, preferred_element_type=jnp.float32)
            + jnp.dot(neigh_mean, w_neigh, preferred_element_type=jnp.float32),
            "feat",
            scatter_dimension=0,
            tiled=True,
        )
        + bias
    )
    activated = jax.nn.elu(pre_act).astype(jnp.bfloat16)
    elu_slope = jnp.where(pre_act > 0, 1.0, jnp.exp(jnp.minimum(pre_act, 0.0)))
    dpre = (d_out.astype(jnp.float32) * elu_slope).astype(jnp.bfloat16)
    dpre_group = lax.all_gather(dpre, "feat", axis=0, tiled=True)
    part_self = lax.dot_general(
        own_rows, dpre_group, (((0,), (0,)), ((), ())), preferred_element_type=jnp.float32
    )
    part_neigh = lax.dot_general(
        neigh_mean, dpre_group, (((0,), (0,)), ((), ())), preferred_element_type=jnp.float32
    )
    sum_self, sum_neigh = lax.psum((part_self, part_neigh), "node")
    d_self = lax.dot_general(
        dpre_group, w_self, (((1,), (1,)), ((), ())), preferred_element_type=jnp.float32
    ).astype(jnp.bfloat16)
    d_neigh = lax.dot_general(
        dpre_group, w_neigh, (((1,), (1,)), ((), ())), preferred_element_type=jnp.float32
    ).astype(jnp.bfloat16)
    grad_scale = 1.0 / math.sqrt(node_total)
    grad_self = sum_self * grad_scale
    grad_neigh = sum_neigh * grad_scale
    d_scaled = (
        d_neigh.astype(jnp.float32).reshape(blocks_here, block_size, feat_cols) / denom[..., None]
    ).astype(jnp.bfloat16)

    def backward_slot(slot_idx, grad_all):
        adjacency, block_ids, live_mask = slot_tiles(slot_idx)
        product = jnp.einsum(
            "bij,bic->bjc", adjacency, d_scaled, preferred_element_type=jnp.float32
        )
        return grad_all.at[block_ids].add(product * live_mask[:, None, None])

    grad_all = lax.fori_loop(
        0, slot_total, backward_slot, jnp.zeros((all_blocks, block_size, feat_cols), jnp.float32)
    )
    flat_grad = grad_all.reshape(node_total, feat_cols)
    group_part = lax.dynamic_slice_in_dim(flat_grad, node_group * group_rows, group_rows, 0)
    flat_grad = lax.dynamic_update_slice_in_dim(
        flat_grad, group_part + d_self.astype(jnp.float32), node_group * group_rows, 0
    )
    grad_features = lax.psum_scatter(flat_grad, "node", scatter_dimension=0, tiled=True)
    return (activated, grad_features, grad_self, grad_neigh)


def solution(mesh):
    placed = (
        P(None, "feat"),
        P("feat", None),
        P("feat", None),
        P(),
        P(("node", "feat"), None),
        P("node", None),
        P("node"),
        P("node", None, None, None),
    )
    return jax.shard_map(
        shards,
        mesh=mesh,
        in_specs=placed,
        out_specs=(P(("node", "feat"), None), P("node", "feat"), P("feat", None), P("feat", None)),
        check_vma=False,
    )
```

profile of v0, /device:TPU:1, one launch (start us, length us, event | category | flops | bytes accessed | tf_op | source)
XLA Modules:
  0.0 586.5 jit_solution(15753192361563251253)
XLA Ops:
  7.3 1.1 copy-done
  8.6 4.6 copy.24
  13.2 101.6 %while.30 = (s32[]{:T(128)}, f32[64,128,16]{1,2,0:T(8,128)S(1)}, f32[64,128]{0,1:T(8,128)S(1)}, s32[64,16,8,128]{3,2,0,1:T(8,128)}, s32[64,16]{0,1:T(8,128)}, /*...) while((s32[]{:T(128)}, f32[64,128,16]{1,2,0:T(8,128)S(1)}, ...), condition=%wide.region_2.3_spmd.clone, body=%wide.region_0.2_spmd.clone.sunk | while | flops 42353984 | bytes 7282812 | solution.py:42
  16.2 1.2 convert_reduce_fusion.2
  18.3 1.2 fusion.66
  22.6 1.2 convert_reduce_fusion.2
  24.7 1.2 fusion.66
  28.9 1.2 convert_reduce_fusion.2
  31.0 1.2 fusion.66
  35.3 1.2 convert_reduce_fusion.2
  37.4 1.2 fusion.66
  41.6 1.2 convert_reduce_fusion.2
  43.7 1.2 fusion.66
  48.0 1.2 convert_reduce_fusion.2
  50.1 1.2 fusion.66
  54.3 1.2 convert_reduce_fusion.2
  56.4 1.2 fusion.66
  60.7 1.2 convert_reduce_fusion.2
  62.8 1.2 fusion.66
  67.0 1.2 convert_reduce_fusion.2
  69.1 1.2 fusion.66
  73.4 1.2 convert_reduce_fusion.2
  75.5 1.2 fusion.66
  79.7 1.2 convert_reduce_fusion.2
  81.8 1.2 fusion.66
  86.1 1.2 convert_reduce_fusion.2
  88.2 1.2 fusion.66
  92.4 1.2 convert_reduce_fusion.2
  94.5 1.2 fusion.66
  98.8 1.2 convert_reduce_fusion.2
  100.9 1.2 fusion.66
  105.1 1.2 convert_reduce_fusion.2
  107.2 1.2 fusion.66
  111.5 1.2 convert_reduce_fusion.2
  113.6 1.2 fusion.66
  114.9 1.3 fusion.22
  116.2 4.5 convolution_add_fusion
  120.8 150.6 %reduce-scatter.3.cloned.1.call-done = f32[128,256]{1,0:T(8,128)} async-done(((f32[8192,256]{1,0:T(8,128)}), f32[128,256]{1,0:T(8,128)}) %reduce-scatter.3.cloned.1.call-update) | async-done | bytes 131088 | tf_op jit(solution)/shard_map/reduce_scatter | solution.py:55
  271.5 1.6 fusion.27
  273.2 84.5 %all-gather.2.cloned.1.call-done = bf16[8192,256]{1,0:T(8,128)(2,1)} async-done(((bf16[128,256]{1,0:T(8,128)(2,1)}), bf16[8192,256]{1,0:T(8,128)(2,1)}) %all-gather.2.cloned.1.call-update) | async-done | bytes 4194320 | tf_op jit(solution)/shard_map/all_gather | solution.py:67
  357.6 3.4 fusion.12
  361.1 1.5 broadcast_in_dim.47
  362.6 181.3 %while.29 = (s32[]{:T(128)}, f32[256,128,16]{1,2,0:T(8,128)}, s32[64,16]{0,1:T(8,128)}, s32[64,16,8,128]{3,2,0,1:T(8,128)}, bf16[64,128,16]{1,2,0:T(8,128)(2,1)S(1)}, /*index=5*/s32[64]{0:T(128)}, s32[]{:T(128)}) while((s32[]{:T(128)}, f32[256,128,16]{1,2,0:T(8,128)}, s32[64,16]{0,1:T(8,128)}, s32[64,16,8,128]{3,2,0,1:T(8,128)}, ...), condition=%wide.region_6.7_spmd, body=%wide.region_4.6_spmd.sunk | while | flops 36962624 | bytes 7343713 | solution.py:95
  366.4 7.5 %scatter_fusion = f32[256,128,16]{1,2,0:T(8,128)} fusion(f32[256,128,16]{1,2,0:T(8,128)} %get-tuple-element.451, s32[64]{0:T(128)S(1)} %fusion.60, f32[64,128,16]{1,2,0:T(8,128)S(1)} %convolution_multiply_fusion.3), kind=kCustom, calls=%fused_computation.1.clone.1 | custom fusion | flops 131072 | bytes 1573120 | tf_op jit(solution)/shard_map/while/body/eval_jaxpr/scatter-add | solution.py:93
  377.7 7.5 %scatter_fusion = f32[256,128,16]{1,2,0:T(8,128)} fusion(f32[256,128,16]{1,2,0:T(8,128)} %get-tuple-element.451, s32[64]{0:T(128)S(1)} %fusion.60, f32[64,128,16]{1,2,0:T(8,128)S(1)} %convolution_multiply_fusion.3), kind=kCustom, calls=%fused_computation.1.clone.1 | custom fusion | flops 131072 | bytes 1573120 | tf_op jit(solution)/shard_map/while/body/eval_jaxpr/scatter-add | solution.py:93
  389.0 7.5 %scatter_fusion = f32[256,128,16]{1,2,0:T(8,128)} fusion(f32[256,128,16]{1,2,0:T(8,128)} %get-tuple-element.451, s32[64]{0:T(128)S(1)} %fusion.60, f32[64,128,16]{1,2,0:T(8,128)S(1)} %convolution_multiply_fusion.3), kind=kCustom, calls=%fused_computation.1.clone.1 | custom fusion | flops 131072 | bytes 1573120 | tf_op jit(solution)/shard_map/while/body/eval_jaxpr/scatter-add | solution.py:93
  400.4 7.5 %scatter_fusion = f32[256,128,16]{1,2,0:T(8,128)} fusion(f32[256,128,16]{1,2,0:T(8,128)} %get-tuple-element.451, s32[64]{0:T(128)S(1)} %fusion.60, f32[64,128,16]{1,2,0:T(8,128)S(1)} %convolution_multiply_fusion.3), kind=kCustom, calls=%fused_computation.1.clone.1 | custom fusion | flops 131072 | bytes 1573120 | tf_op jit(solution)/shard_map/while/body/eval_jaxpr/scatter-add | solution.py:93
  411.7 7.5 %scatter_fusion = f32[256,128,16]{1,2,0:T(8,128)} fusion(f32[256,128,16]{1,2,0:T(8,128)} %get-tuple-element.451, s32[64]{0:T(128)S(1)} %fusion.60, f32[64,128,16]{1,2,0:T(8,128)S(1)} %convolution_multiply_fusion.3), kind=kCustom, calls=%fused_computation.1.clone.1 | custom fusion | flops 131072 | bytes 1573120 | tf_op jit(solution)/shard_map/while/body/eval_jaxpr/scatter-add | solution.py:93
  423.0 7.5 %scatter_fusion = f32[256,128,16]{1,2,0:T(8,128)} fusion(f32[256,128,16]{1,2,0:T(8,128)} %get-tuple-element.451, s32[64]{0:T(128)S(1)} %fusion.60, f32[64,128,16]{1,2,0:T(8,128)S(1)} %convolution_multiply_fusion.3), kind=kCustom, calls=%fused_computation.1.clone.1 | custom fusion | flops 131072 | bytes 1573120 | tf_op jit(solution)/shard_map/while/body/eval_jaxpr/scatter-add | solution.py:93
  434.4 7.5 %scatter_fusion = f32[256,128,16]{1,2,0:T(8,128)} fusion(f32[256,128,16]{1,2,0:T(8,128)} %get-tuple-element.451, s32[64]{0:T(128)S(1)} %fusion.60, f32[64,128,16]{1,2,0:T(8,128)S(1)} %convolution_multiply_fusion.3), kind=kCustom, calls=%fused_computation.1.clone.1 | custom fusion | flops 131072 | bytes 1573120 | tf_op jit(solution)/shard_map/while/body/eval_jaxpr/scatter-add | solution.py:93
  445.7 7.5 %scatter_fusion = f32[256,128,16]{1,2,0:T(8,128)} fusion(f32[256,128,16]{1,2,0:T(8,128)} %get-tuple-element.451, s32[64]{0:T(128)S(1)} %fusion.60, f32[64,128,16]{1,2,0:T(8,128)S(1)} %convolution_multiply_fusion.3), kind=kCustom, calls=%fused_computation.1.clone.1 | custom fusion | flops 131072 | bytes 1573120 | tf_op jit(solution)/shard_map/while/body/eval_jaxpr/scatter-add | solution.py:93
  457.0 7.5 %scatter_fusion = f32[256,128,16]{1,2,0:T(8,128)} fusion(f32[256,128,16]{1,2,0:T(8,128)} %get-tuple-element.451, s32[64]{0:T(128)S(1)} %fusion.60, f32[64,128,16]{1,2,0:T(8,128)S(1)} %convolution_multiply_fusion.3), kind=kCustom, calls=%fused_computation.1.clone.1 | custom fusion | flops 131072 | bytes 1573120 | tf_op jit(solution)/shard_map/while/body/eval_jaxpr/scatter-add | solution.py:93
  468.4 7.5 %scatter_fusion = f32[256,128,16]{1,2,0:T(8,128)} fusion(f32[256,128,16]{1,2,0:T(8,128)} %get-tuple-element.451, s32[64]{0:T(128)S(1)} %fusion.60, f32[64,128,16]{1,2,0:T(8,128)S(1)} %convolution_multiply_fusion.3), kind=kCustom, calls=%fused_computation.1.clone.1 | custom fusion | flops 131072 | bytes 1573120 | tf_op jit(solution)/shard_map/while/body/eval_jaxpr/scatter-add | solution.py:93
  479.7 7.5 %scatter_fusion = f32[256,128,16]{1,2,0:T(8,128)} fusion(f32[256,128,16]{1,2,0:T(8,128)} %get-tuple-element.451, s32[64]{0:T(128)S(1)} %fusion.60, f32[64,128,16]{1,2,0:T(8,128)S(1)} %convolution_multiply_fusion.3), kind=kCustom, calls=%fused_computation.1.clone.1 | custom fusion | flops 131072 | bytes 1573120 | tf_op jit(solution)/shard_map/while/body/eval_jaxpr/scatter-add | solution.py:93
  491.0 7.5 %scatter_fusion = f32[256,128,16]{1,2,0:T(8,128)} fusion(f32[256,128,16]{1,2,0:T(8,128)} %get-tuple-element.451, s32[64]{0:T(128)S(1)} %fusion.60, f32[64,128,16]{1,2,0:T(8,128)S(1)} %convolution_multiply_fusion.3), kind=kCustom, calls=%fused_computation.1.clone.1 | custom fusion | flops 131072 | bytes 1573120 | tf_op jit(solution)/shard_map/while/body/eval_jaxpr/scatter-add | solution.py:93
  502.4 7.5 %scatter_fusion = f32[256,128,16]{1,2,0:T(8,128)} fusion(f32[256,128,16]{1,2,0:T(8,128)} %get-tuple-element.451, s32[64]{0:T(128)S(1)} %fusion.60, f32[64,128,16]{1,2,0:T(8,128)S(1)} %convolution_multiply_fusion.3), kind=kCustom, calls=%fused_computation.1.clone.1 | custom fusion | flops 131072 | bytes 1573120 | tf_op jit(solution)/shard_map/while/body/eval_jaxpr/scatter-add | solution.py:93
  513.7 7.5 %scatter_fusion = f32[256,128,16]{1,2,0:T(8,128)} fusion(f32[256,128,16]{1,2,0:T(8,128)} %get-tuple-element.451, s32[64]{0:T(128)S(1)} %fusion.60, f32[64,128,16]{1,2,0:T(8,128)S(1)} %convolution_multiply_fusion.3), kind=kCustom, calls=%fused_computation.1.clone.1 | custom fusion | flops 131072 | bytes 1573120 | tf_op jit(solution)/shard_map/while/body/eval_jaxpr/scatter-add | solution.py:93
  525.0 7.5 %scatter_fusion = f32[256,128,16]{1,2,0:T(8,128)} fusion(f32[256,128,16]{1,2,0:T(8,128)} %get-tuple-element.451, s32[64]{0:T(128)S(1)} %fusion.60, f32[64,128,16]{1,2,0:T(8,128)S(1)} %convolution_multiply_fusion.3), kind=kCustom, calls=%fused_computation.1.clone.1 | custom fusion | flops 131072 | bytes 1573120 | tf_op jit(solution)/shard_map/while/body/eval_jaxpr/scatter-add | solution.py:93
  536.4 7.5 %scatter_fusion = f32[256,128,16]{1,2,0:T(8,128)} fusion(f32[256,128,16]{1,2,0:T(8,128)} %get-tuple-element.451, s32[64]{0:T(128)S(1)} %fusion.60, f32[64,128,16]{1,2,0:T(8,128)S(1)} %convolution_multiply_fusion.3), kind=kCustom, calls=%fused_computation.1.clone.1 | custom fusion | flops 131072 | bytes 1573120 | tf_op jit(solution)/shard_map/while/body/eval_jaxpr/scatter-add | solution.py:93
  543.9 3.2 copy_bitcast_fusion
  547.1 3.0 fusion.10
  550.1 3.0 fusion.20
  554.2 14.9 %all-reduce = (f32[16,256]{1,0:T(8,128)S(1)}, f32[16,256]{1,0:T(8,128)S(1)}) all-reduce(f32[16,256]{1,0:T(8,128)S(1)} %fusion.20, f32[16,256]{1,0:T(8,128)S(1)} %fusion.14), channel_id=1, replica_groups=mesh['feat'=64,'node'=4] {'node'}, use_global_device_ids=true, to_apply=%region_8.9 | all-reduce | flops 8192 | bytes 65536 | tf_op jit(solution)/shard_map/psum | solution.py:74
  569.7 10.2 %reduce-scatter.5.cloned.1.call-done = f32[8192,16]{0,1:T(8,128)} async-done(((f32[32768,16]{0,1:T(8,128)}), f32[8192,16]{0,1:T(8,128)}) %reduce-scatter.5.cloned.1.call-update) | async-done | bytes 524304 | tf_op jit(solution)/shard_map/reduce_scatter | solution.py:103
  (299 shorter events, 126.5 us)
Async XLA Ops:
  7.2 1.2 copy-start
  7.2 264.3 %reduce-scatter.3.cloned.1.call-start = ((), (), s32[]{:S(2)}) async-start(), calls=%async_computation.2 | async-start | bytes 8519680 | tf_op jit(solution)/shard_map/reduce_scatter | solution.py:55
  13.2 101.7 %copy-start.5 = (bf16[16,256]{1,0:T(8,128)(2,1)S(1)}, bf16[16,256]{1,0:T(8,128)(2,1)}, u32[]{:S(2)}) copy-start(bf16[16,256]{1,0:T(8,128)(2,1)} %param.13) | copy-start | bytes 24580
  114.9 1.3 copy-start.4
  120.7 150.7 %copy-start.3 = (bf16[128,256]{1,0:T(8,128)(2,1)S(1)}, bf16[128,256]{1,0:T(8,128)(2,1)}, u32[]{:S(2)}) copy-start(bf16[128,256]{1,0:T(8,128)(2,1)} %param.16) | copy-start | bytes 196612
  120.7 150.7 %copy-start.6 = (f32[256]{0:T(256)S(1)}, f32[256]{0:T(256)}, u32[]{:S(2)}) copy-start(f32[256]{0:T(256)} %param.15) | copy-start | bytes 3076
  120.8 236.9 %all-gather.2.cloned.1.call-start = ((), (), s32[]{:S(2)}) async-start(), calls=%async_computation.3 | async-start | bytes 4259840 | tf_op jit(solution)/shard_map/all_gather | solution.py:67
  273.1 306.8 %reduce-scatter.5.cloned.1.call-start = ((), (), s32[]{:S(2)}) async-start(), calls=%async_computation.4 | async-start | bytes 2621440 | tf_op jit(solution)/shard_map/reduce_scatter | solution.py:103
  543.9 3.2 copy-start.1
  550.1 3.5 copy-start.2
Sparse Core Ops, SparseCore 0:
  120.9 150.5 reduce-scatter.2
  275.2 82.3 all-gather.1
  550.2 29.6 reduce-scatter.4
where the time goes:
time: 592 us; the launch traced here: 586 us
  waiting for transfers between devices  245 us (41%)
  other arithmetic  209 us (35%)
  local copies, waits for them, and re-layouts  57 us (10%)
  matrix products  45.7 us (8%)
  blocking collectives  14.9 us (3%)
  between operations  13.8 us (2%)
    reduce_scatter x1, waiting for transfers between devices, shards(): lax.psum_scatter(jnp.dot(own_rows, w_self, preferred_element_type=jnp.flo...  151 us
    scatter-add x16, other arithmetic, backward_slot(): return grad_all.at[block_ids].add(product * live_mask[:, None, None])  120 us
    all_gather x1, waiting for transfers between devices, shards(): dpre_group = lax.all_gather(dpre, 'feat', axis=0, tiled=True)  84.5 us
    shift_right_arithmetic x96, local copies, waits for them, and re-layouts, unpack(): jnp.right_shift(packed[..., :, None, :], shifts[:, None])  33.8 us
    convert_element_type x32, other arithmetic, slot_tiles(): adjacency = unpack(packed).astype(jnp.bfloat16)  23.8 us
    convert_element_type x32, other arithmetic, slot_tiles(): live_mask = (slot_idx < nbr_count).astype(jnp.float32)  21.2 us
    dot_general x16, matrix products, forward_slot(): jnp.einsum('bij,bjc->bic', adjacency, source, preferred_element_type=jnp....  19.2 us
    reduce_sum x16, other arithmetic, forward_slot(): jnp.sum(adjacency, axis=2, dtype=jnp.float32) * live_mask[:, None]  18.5 us
  transfers between devices with their start and end apart: 3, of which 3 were waited for; matrix products, arithmetic and copies ran while one was open for 1% of the time, Pallas kernels for 0%

commit v1 on v0

--- a/solution.py
+++ b/solution.py
@@ -3,6 +3,13 @@
 import jax.numpy as jnp
 from jax import lax
 from jax.sharding import PartitionSpec as P
+
+
+def exchange_gather(x, axis, dim):
+    peers = lax.axis_size(axis)
+    blocks = jnp.stack([x for _ in range(peers)])
+    blocks = lax.all_to_all(blocks, axis, split_axis=0, concat_axis=0)
+    return jnp.concatenate(blocks, axis=dim)
 
 
 def unpack(packed):
@@ -64,7 +71,7 @@
     activated = jax.nn.elu(pre_act).astype(jnp.bfloat16)
     elu_slope = jnp.where(pre_act > 0, 1.0, jnp.exp(jnp.minimum(pre_act, 0.0)))
     dpre = (d_out.astype(jnp.float32) * elu_slope).astype(jnp.bfloat16)
-    dpre_group = lax.all_gather(dpre, "feat", axis=0, tiled=True)
+    dpre_group = exchange_gather(dpre, "feat", 0)
     part_self = lax.dot_general(
         own_rows, dpre_group, (((0,), (0,)), ((), ())), preferred_element_type=jnp.float32
     )

time: 592 us -> 614 us (1.037)
  blocking collectives: 14.9 us -> 123 us
  waiting for transfers between devices: 245 us -> 161 us
    all_to_all x0 -> x1, blocking collectives: none -> 108 us  [exchange_gather(): blocks = lax.all_to_all(blocks, axis, split_axis=0, concat_axis=0)]
    all_gather x1 -> x0, waiting for transfers between devices: 84.5 us -> none  [shards(): dpre_group = lax.all_gather(dpre, 'feat', axis=0, tiled=True)]
  transfers between devices with their start and end apart: 3 -> 2, of which waited for: 3 -> 2; matrix products, arithmetic and copies ran while one was open for 1% -> 1% of each run, Pallas kernels for 0% -> 0%
where the time goes in v1:
time: 614 us; the launch traced here: 609 us
  other arithmetic  209 us (34%)
  waiting for transfers between devices  161 us (26%)
  blocking collectives  123 us (20%)
  local copies, waits for them, and re-layouts  57.5 us (9%)
  matrix products  43.5 us (7%)
  between operations  14.1 us (2%)
    reduce_scatter x1, waiting for transfers between devices, shards(): lax.psum_scatter(jnp.dot(own_rows, w_self, preferred_element_type=jnp.flo...  151 us
    scatter-add x16, other arithmetic, backward_slot(): return grad_all.at[block_ids].add(product * live_mask[:, None, None])  120 us
    all_to_all x1, blocking collectives, exchange_gather(): blocks = lax.all_to_all(blocks, axis, split_axis=0, concat_axis=0)  108 us
    shift_right_arithmetic x96, local copies, waits for them, and re-layouts, unpack(): jnp.right_shift(packed[..., :, None, :], shifts[:, None])  33.8 us
    convert_element_type x32, other arithmetic, slot_tiles(): adjacency = unpack(packed).astype(jnp.bfloat16)  23.8 us
    convert_element_type x32, other arithmetic, slot_tiles(): live_mask = (slot_idx < nbr_count).astype(jnp.float32)  21.2 us
    dot_general x16, matrix products, forward_slot(): jnp.einsum('bij,bjc->bic', adjacency, source, preferred_element_type=jnp....  19.2 us
    reduce_sum x16, other arithmetic, forward_slot(): jnp.sum(adjacency, axis=2, dtype=jnp.float32) * live_mask[:, None]  18.5 us
  transfers between devices with their start and end apart: 2, of which 2 were waited for; matrix products, arithmetic and copies ran while one was open for 1% of the time, Pallas kernels for 0%

profile of v1, /device:TPU:1, one launch (start us, length us, event | category | flops | bytes accessed | tf_op | source)
XLA Modules:
  0.0 608.5 jit_solution(3825650630199922125)
XLA Ops:
  7.3 1.1 copy-done
  8.6 4.6 copy.24
  13.1 101.6 %while.30 = (s32[]{:T(128)}, f32[64,128,16]{1,2,0:T(8,128)S(1)}, f32[64,128]{0,1:T(8,128)S(1)}, s32[64,16,8,128]{3,2,0,1:T(8,128)}, s32[64,16]{0,1:T(8,128)}, /*...) while((s32[]{:T(128)}, f32[64,128,16]{1,2,0:T(8,128)S(1)}, ...), condition=%wide.region_2.3_spmd.clone, body=%wide.region_0.2_spmd.clone.sunk | while | flops 42353984 | bytes 7282812 | solution.py:49
  16.2 1.2 convert_reduce_fusion.2
  18.3 1.2 fusion.61
  22.6 1.2 convert_reduce_fusion.2
  24.6 1.2 fusion.61
  28.9 1.2 convert_reduce_fusion.2
  31.0 1.2 fusion.61
  35.3 1.2 convert_reduce_fusion.2
  37.3 1.2 fusion.61
  41.6 1.2 convert_reduce_fusion.2
  43.7 1.2 fusion.61
  48.0 1.2 convert_reduce_fusion.2
  50.0 1.2 fusion.61
  54.3 1.2 convert_reduce_fusion.2
  56.4 1.2 fusion.61
  60.7 1.2 convert_reduce_fusion.2
  62.7 1.2 fusion.61
  67.0 1.2 convert_reduce_fusion.2
  69.1 1.2 fusion.61
  73.4 1.2 convert_reduce_fusion.2
  75.4 1.2 fusion.61
  79.7 1.2 convert_reduce_fusion.2
  81.8 1.2 fusion.61
  86.1 1.2 convert_reduce_fusion.2
  88.1 1.2 fusion.61
  92.4 1.2 convert_reduce_fusion.2
  94.5 1.2 fusion.61
  98.8 1.2 convert_reduce_fusion.2
  100.8 1.2 fusion.61
  105.1 1.2 convert_reduce_fusion.2
  107.2 1.2 fusion.61
  111.5 1.2 convert_reduce_fusion.2
  113.5 1.2 fusion.61
  114.9 1.3 fusion.18
  116.2 4.5 convolution_add_fusion
  120.8 150.8 %reduce-scatter.3.cloned.1.call-done = f32[128,256]{1,0:T(8,128)} async-done(((f32[8192,256]{1,0:T(8,128)}), f32[128,256]{1,0:T(8,128)}) %reduce-scatter.3.cloned.1.call-update) | async-done | bytes 131088 | tf_op jit(solution)/shard_map/reduce_scatter | solution.py:62
  271.6 1.6 fusion.23
  273.7 108.3 %all_to_all.5 = bf16[64,128,256]{2,1,0:T(8,128)(2,1)S(1)} all-to-all(bf16[64,128,256]{2,1,0:T(8,128)(2,1)S(1)} %stack.2), channel_id=1, replica_groups=mesh['feat'=64,'node'=4] {'feat'}, dimensions={0} | all-to-all | bytes 8388608 | tf_op jit(solution)/shard_map/all_to_all | solution.py:11
  382.0 1.2 fusion.12
  383.3 1.5 broadcast_in_dim.47
  384.8 181.3 %while.29 = (s32[]{:T(128)}, f32[256,128,16]{1,2,0:T(8,128)}, s32[64,16]{0,1:T(8,128)}, s32[64,16,8,128]{3,2,0,1:T(8,128)}, bf16[64,128,16]{1,2,0:T(8,128)(2,1)S(1)}, /*index=5*/s32[64]{0:T(128)}, s32[]{:T(128)}) while((s32[]{:T(128)}, f32[256,128,16]{1,2,0:T(8,128)}, s32[64,16]{0,1:T(8,128)}, s32[64,16,8,128]{3,2,0,1:T(8,128)}, ...), condition=%wide.region_6.7_spmd, body=%wide.region_4.6_spmd.sunk | while | flops 36962624 | bytes 7343713 | solution.py:102
  388.6 7.5 %scatter_fusion = f32[256,128,16]{1,2,0:T(8,128)} fusion(f32[256,128,16]{1,2,0:T(8,128)} %get-tuple-element.451, s32[64]{0:T(128)S(1)} %fusion.55, f32[64,128,16]{1,2,0:T(8,128)S(1)} %convolution_multiply_fusion.3), kind=kCustom, calls=%fused_computation.1.clone.1 | custom fusion | flops 131072 | bytes 1573120 | tf_op jit(solution)/shard_map/while/body/eval_jaxpr/scatter-add | solution.py:100
  399.9 7.5 %scatter_fusion = f32[256,128,16]{1,2,0:T(8,128)} fusion(f32[256,128,16]{1,2,0:T(8,128)} %get-tuple-element.451, s32[64]{0:T(128)S(1)} %fusion.55, f32[64,128,16]{1,2,0:T(8,128)S(1)} %convolution_multiply_fusion.3), kind=kCustom, calls=%fused_computation.1.clone.1 | custom fusion | flops 131072 | bytes 1573120 | tf_op jit(solution)/shard_map/while/body/eval_jaxpr/scatter-add | solution.py:100
  411.3 7.5 %scatter_fusion = f32[256,128,16]{1,2,0:T(8,128)} fusion(f32[256,128,16]{1,2,0:T(8,128)} %get-tuple-element.451, s32[64]{0:T(128)S(1)} %fusion.55, f32[64,128,16]{1,2,0:T(8,128)S(1)} %convolution_multiply_fusion.3), kind=kCustom, calls=%fused_computation.1.clone.1 | custom fusion | flops 131072 | bytes 1573120 | tf_op jit(solution)/shard_map/while/body/eval_jaxpr/scatter-add | solution.py:100
  422.6 7.5 %scatter_fusion = f32[256,128,16]{1,2,0:T(8,128)} fusion(f32[256,128,16]{1,2,0:T(8,128)} %get-tuple-element.451, s32[64]{0:T(128)S(1)} %fusion.55, f32[64,128,16]{1,2,0:T(8,128)S(1)} %convolution_multiply_fusion.3), kind=kCustom, calls=%fused_computation.1.clone.1 | custom fusion | flops 131072 | bytes 1573120 | tf_op jit(solution)/shard_map/while/body/eval_jaxpr/scatter-add | solution.py:100
  433.9 7.5 %scatter_fusion = f32[256,128,16]{1,2,0:T(8,128)} fusion(f32[256,128,16]{1,2,0:T(8,128)} %get-tuple-element.451, s32[64]{0:T(128)S(1)} %fusion.55, f32[64,128,16]{1,2,0:T(8,128)S(1)} %convolution_multiply_fusion.3), kind=kCustom, calls=%fused_computation.1.clone.1 | custom fusion | flops 131072 | bytes 1573120 | tf_op jit(solution)/shard_map/while/body/eval_jaxpr/scatter-add | solution.py:100
  445.3 7.5 %scatter_fusion = f32[256,128,16]{1,2,0:T(8,128)} fusion(f32[256,128,16]{1,2,0:T(8,128)} %get-tuple-element.451, s32[64]{0:T(128)S(1)} %fusion.55, f32[64,128,16]{1,2,0:T(8,128)S(1)} %convolution_multiply_fusion.3), kind=kCustom, calls=%fused_computation.1.clone.1 | custom fusion | flops 131072 | bytes 1573120 | tf_op jit(solution)/shard_map/while/body/eval_jaxpr/scatter-add | solution.py:100
  456.6 7.5 %scatter_fusion = f32[256,128,16]{1,2,0:T(8,128)} fusion(f32[256,128,16]{1,2,0:T(8,128)} %get-tuple-element.451, s32[64]{0:T(128)S(1)} %fusion.55, f32[64,128,16]{1,2,0:T(8,128)S(1)} %convolution_multiply_fusion.3), kind=kCustom, calls=%fused_computation.1.clone.1 | custom fusion | flops 131072 | bytes 1573120 | tf_op jit(solution)/shard_map/while/body/eval_jaxpr/scatter-add | solution.py:100
  467.9 7.5 %scatter_fusion = f32[256,128,16]{1,2,0:T(8,128)} fusion(f32[256,128,16]{1,2,0:T(8,128)} %get-tuple-element.451, s32[64]{0:T(128)S(1)} %fusion.55, f32[64,128,16]{1,2,0:T(8,128)S(1)} %convolution_multiply_fusion.3), kind=kCustom, calls=%fused_computation.1.clone.1 | custom fusion | flops 131072 | bytes 1573120 | tf_op jit(solution)/shard_map/while/body/eval_jaxpr/scatter-add | solution.py:100
  479.3 7.5 %scatter_fusion = f32[256,128,16]{1,2,0:T(8,128)} fusion(f32[256,128,16]{1,2,0:T(8,128)} %get-tuple-element.451, s32[64]{0:T(128)S(1)} %fusion.55, f32[64,128,16]{1,2,0:T(8,128)S(1)} %convolution_multiply_fusion.3), kind=kCustom, calls=%fused_computation.1.clone.1 | custom fusion | flops 131072 | bytes 1573120 | tf_op jit(solution)/shard_map/while/body/eval_jaxpr/scatter-add | solution.py:100
  490.6 7.5 %scatter_fusion = f32[256,128,16]{1,2,0:T(8,128)} fusion(f32[256,128,16]{1,2,0:T(8,128)} %get-tuple-element.451, s32[64]{0:T(128)S(1)} %fusion.55, f32[64,128,16]{1,2,0:T(8,128)S(1)} %convolution_multiply_fusion.3), kind=kCustom, calls=%fused_computation.1.clone.1 | custom fusion | flops 131072 | bytes 1573120 | tf_op jit(solution)/shard_map/while/body/eval_jaxpr/scatter-add | solution.py:100
  501.9 7.5 %scatter_fusion = f32[256,128,16]{1,2,0:T(8,128)} fusion(f32[256,128,16]{1,2,0:T(8,128)} %get-tuple-element.451, s32[64]{0:T(128)S(1)} %fusion.55, f32[64,128,16]{1,2,0:T(8,128)S(1)} %convolution_multiply_fusion.3), kind=kCustom, calls=%fused_computation.1.clone.1 | custom fusion | flops 131072 | bytes 1573120 | tf_op jit(solution)/shard_map/while/body/eval_jaxpr/scatter-add | solution.py:100
  513.3 7.5 %scatter_fusion = f32[256,128,16]{1,2,0:T(8,128)} fusion(f32[256,128,16]{1,2,0:T(8,128)} %get-tuple-element.451, s32[64]{0:T(128)S(1)} %fusion.55, f32[64,128,16]{1,2,0:T(8,128)S(1)} %convolution_multiply_fusion.3), kind=kCustom, calls=%fused_computation.1.clone.1 | custom fusion | flops 131072 | bytes 1573120 | tf_op jit(solution)/shard_map/while/body/eval_jaxpr/scatter-add | solution.py:100
  524.6 7.5 %scatter_fusion = f32[256,128,16]{1,2,0:T(8,128)} fusion(f32[256,128,16]{1,2,0:T(8,128)} %get-tuple-element.451, s32[64]{0:T(128)S(1)} %fusion.55, f32[64,128,16]{1,2,0:T(8,128)S(1)} %convolution_multiply_fusion.3), kind=kCustom, calls=%fused_computation.1.clone.1 | custom fusion | flops 131072 | bytes 1573120 | tf_op jit(solution)/shard_map/while/body/eval_jaxpr/scatter-add | solution.py:100
  535.9 7.5 %scatter_fusion = f32[256,128,16]{1,2,0:T(8,128)} fusion(f32[256,128,16]{1,2,0:T(8,128)} %get-tuple-element.451, s32[64]{0:T(128)S(1)} %fusion.55, f32[64,128,16]{1,2,0:T(8,128)S(1)} %convolution_multiply_fusion.3), kind=kCustom, calls=%fused_computation.1.clone.1 | custom fusion | flops 131072 | bytes 1573120 | tf_op jit(solution)/shard_map/while/body/eval_jaxpr/scatter-add | solution.py:100
  547.2 7.5 %scatter_fusion = f32[256,128,16]{1,2,0:T(8,128)} fusion(f32[256,128,16]{1,2,0:T(8,128)} %get-tuple-element.451, s32[64]{0:T(128)S(1)} %fusion.55, f32[64,128,16]{1,2,0:T(8,128)S(1)} %convolution_multiply_fusion.3), kind=kCustom, calls=%fused_computation.1.clone.1 | custom fusion | flops 131072 | bytes 1573120 | tf_op jit(solution)/shard_map/while/body/eval_jaxpr/scatter-add | solution.py:100
  558.6 7.5 %scatter_fusion = f32[256,128,16]{1,2,0:T(8,128)} fusion(f32[256,128,16]{1,2,0:T(8,128)} %get-tuple-element.451, s32[64]{0:T(128)S(1)} %fusion.55, f32[64,128,16]{1,2,0:T(8,128)S(1)} %convolution_multiply_fusion.3), kind=kCustom, calls=%fused_computation.1.clone.1 | custom fusion | flops 131072 | bytes 1573120 | tf_op jit(solution)/shard_map/while/body/eval_jaxpr/scatter-add | solution.py:100
  566.1 3.2 copy_bitcast_fusion
  569.3 3.0 fusion.10
  572.3 3.0 fusion.16
  576.4 15.0 %all-reduce = (f32[16,256]{1,0:T(8,128)S(1)}, f32[16,256]{1,0:T(8,128)S(1)}) all-reduce(f32[16,256]{1,0:T(8,128)S(1)} %fusion.16, f32[16,256]{1,0:T(8,128)S(1)} %convolution_bitcast_fusion), channel_id=1, replica_groups=mesh['feat'=64,'node'=4] {'node'}, use_global_device_ids=true, to_apply=%region_8.9 | all-reduce | flops 8192 | bytes 65536 | tf_op jit(solution)/shard_map/psum | solution.py:81
  592.0 9.6 %reduce-scatter.5.cloned.1.call-done = f32[8192,16]{0,1:T(8,128)} async-done(((f32[32768,16]{0,1:T(8,128)}), f32[8192,16]{0,1:T(8,128)}) %reduce-scatter.5.cloned.1.call-update) | async-done | bytes 524304 | tf_op jit(solution)/shard_map/reduce_scatter | solution.py:110
  (300 shorter events, 126.9 us)
Async XLA Ops:
  7.2 1.2 copy-start
  7.2 264.4 %reduce-scatter.3.cloned.1.call-start = ((), (), s32[]{:S(2)}) async-start(), calls=%async_computation.3 | async-start | bytes 8519680 | tf_op jit(solution)/shard_map/reduce_scatter | solution.py:62
  13.1 101.7 %copy-start.6 = (bf16[16,256]{1,0:T(8,128)(2,1)S(1)}, bf16[16,256]{1,0:T(8,128)(2,1)}, u32[]{:S(2)}) copy-start(bf16[16,256]{1,0:T(8,128)(2,1)} %param.13) | copy-start | bytes 24580
  114.8 1.3 copy-start.5
  120.7 150.9 %copy-start.4 = (bf16[128,256]{1,0:T(8,128)(2,1)S(1)}, bf16[128,256]{1,0:T(8,128)(2,1)}, u32[]{:S(2)}) copy-start(bf16[128,256]{1,0:T(8,128)(2,1)} %param.16) | copy-start | bytes 196612
  120.7 150.9 %copy-start.7 = (f32[256]{0:T(256)S(1)}, f32[256]{0:T(256)}, u32[]{:S(2)}) copy-start(f32[256]{0:T(256)} %param.15) | copy-start | bytes 3076
  120.7 481.0 %reduce-scatter.5.cloned.1.call-start = ((), (), s32[]{:S(2)}) async-start(), calls=%async_computation.4 | async-start | bytes 2621440 | tf_op jit(solution)/shard_map/reduce_scatter | solution.py:110
  382.0 2.7 copy-start.1
  566.1 3.2 copy-start.2
  572.3 3.5 copy-start.3
Sparse Core Ops, SparseCore 0:
  120.8 150.7 reduce-scatter.2
  572.4 29.2 reduce-scatter.4
